TPU v7x, 32 devices: a whole 2x2x4 slice. The times are simulated.
32 devices in a mesh: groups: 2 (over y), dp: 8 (over z, x), section: 2 (over core).
Axes of the slice: x: 2, y: 2, z: 4, core: 2. Of those that a mesh axis runs over, the one named last changes fastest.
Arguments:
- boundary: bfloat16 [2, 32, 64, 8192], P('section', ('groups', 'dp')), parts along dimension 1, may hold values from -6 to 6
- w_query: bfloat16 [2, 8192, 128], P('section', 'dp'), may hold values from -8 to 8
- w_key: bfloat16 [2, 8192, 128], P('section', 'dp'), may hold values from -1 to 1
- w_value: bfloat16 [2, 8192, 128], P('section', 'dp'), may hold values from -0.0625 to 0.0625
- w_out: bfloat16 [2, 128, 8192], P('section', None, 'dp'), may hold values from -0.5 to 0.5
- norm_gain: bfloat16 [2, 8192], P('section'), may hold values from 0.099609375 to 1.8984375
- proj_wide: bfloat16 [64, 8192], replicated, may hold values from -0.0625 to 0.0625
- proj_head: bfloat16 [2, 2, 64, 128], P('section'), may hold values from -0.5 to 0.5
- lengths: int32 [32], P(('groups', 'dp')), parts along dimension 0, may hold values from 1 to 64, 614 in all
- owners: int32 [32, 1], P(('groups', 'dp')), parts along dimension 0, may hold values from 0 to 7; in each aligned block of 16 rows (0 to 15, 16 to 31, ...) at most 4 rows name the same one
Outputs:
- store: bfloat16 [64, 2, 2, 64, 64], P(('groups', 'dp'), 'section'), parts along dimension 0
There are 2 independent parts, one for each index of `groups`. A program takes and returns all parts, laid end to end along the dimension named above; an argument that names none is the same for every part. Nothing has to cross between parts.
Inputs may be any that keep to these rules, and one draw needn't show every extreme that they name: `owners`: every owner is named by at most 4 examples, a bound that some block reaches. `lengths`: some sequence has exactly 64 tokens.
All inputs are finite; a program needn't handle non-finite values. No bound on the sum of `lengths` on one device may be relied on, other than what follows from the above.
Results may differ from a plain program's by a relative error of at most 0.013.
Values may be sent and summed in bfloat16 or wider, within the bound.
A program may use at most 128 MiB of HBM per device.

v0:
```python
import jax
import jax.numpy as jnp
from jax import lax
from jax.sharding import PartitionSpec as P

CAP = 4


EPSILON = 1e-05
MASKED = -1e30


def passed_along(array, axis, by):
    size = lax.axis_size(axis)
    pairs = [(i, i + by) for i in range(size) if 0 <= i + by < size]
    return lax.ppermute(array, axis, pairs)


def for_sending(array):

    def short(part):
        return part.astype(jnp.bfloat16) if part.dtype == jnp.float32 else part

    return jax.tree.map(short, array)


def section_forward(hidden, zero_probe, w_query, w_key, w_value, w_out, section_gain, seq_length):
    token_count = hidden.shape[0]
    head_size = w_query.shape[1]
    widened = hidden.astype(jnp.float32)
    inverse_rms = lax.rsqrt(jnp.mean(widened * widened, axis=-1, keepdims=True) + EPSILON)
    normed = (widened * inverse_rms * section_gain.astype(jnp.float32)).astype(jnp.bfloat16)
    queries = jnp.dot(normed, w_query, preferred_element_type=jnp.float32).astype(jnp.bfloat16)
    key_vecs = jnp.dot(normed, w_key, preferred_element_type=jnp.float32).astype(jnp.bfloat16)
    values = (
        jnp.dot(normed, w_value, preferred_element_type=jnp.float32).astype(jnp.bfloat16)
        + zero_probe
    )
    scores = lax.dot_general(
        queries, key_vecs, (((1,), (1,)), ((), ())), preferred_element_type=jnp.float32
    ) * head_size ** (-0.5)
    positions = jnp.arange(token_count)
    allowed = (positions[None, :] <= positions[:, None]) & (positions[None, :] < seq_length)
    scores = jnp.where(allowed, scores, MASKED)
    highest = jnp.max(scores, axis=-1, keepdims=True)
    expd = jnp.exp(scores - highest)
    probs = (expd / jnp.sum(expd, axis=-1, keepdims=True)).astype(jnp.bfloat16)
    mixed = jnp.dot(probs, values, preferred_element_type=jnp.float32).astype(jnp.bfloat16)
    result = (widened + jnp.dot(mixed, w_out, preferred_element_type=jnp.float32)).astype(
        jnp.bfloat16
    )
    return (result, (normed, mixed))


def module_blocks(normed, mixed, value_grad, cotangent, proj_wide, head_proj, valid):
    contract = (((1,), (1,)), ((), ()))
    across = (((0,), (0,)), ((), ()))
    valid_col = valid[:, None]
    wide_in = lax.dot_general(
        normed, proj_wide, contract, preferred_element_type=jnp.float32
    ).astype(jnp.bfloat16)
    head_in = lax.dot_general(
        mixed, head_proj[1], contract, preferred_element_type=jnp.float32
    ).astype(jnp.bfloat16)
    value_side = jnp.where(
        valid_col,
        lax.dot_general(value_grad, head_proj[0], contract, preferred_element_type=jnp.float32),
        0.0,
    ).astype(jnp.bfloat16)
    wide_out = jnp.where(
        valid_col,
        lax.dot_general(cotangent, proj_wide, contract, preferred_element_type=jnp.float32),
        0.0,
    ).astype(jnp.bfloat16)
    block_value = lax.dot_general(value_side, wide_in, across, preferred_element_type=jnp.float32)
    block_output = lax.dot_general(wide_out, head_in, across, preferred_element_type=jnp.float32)
    return jnp.stack([block_value, block_output]).astype(jnp.bfloat16)


def shards(
    boundary, w_query, w_key, w_value, w_out, norm_gain, proj_wide, proj_head, lengths, owners
):
    my_section = lax.axis_index("section")
    section_count = lax.axis_size("section")
    my_owner = lax.axis_index("dp")
    micro_count = boundary.shape[1]
    token_count = boundary.shape[2]
    model_width = boundary.shape[3]
    proj_rank = proj_wide.shape[0]
    query_w, key_w, value_w, out_w = (
        lax.all_gather(w_query[0], "dp", axis=0, tiled=True),
        lax.all_gather(w_key[0], "dp", axis=0, tiled=True),
        lax.all_gather(w_value[0], "dp", axis=0, tiled=True),
        lax.all_gather(w_out[0], "dp", axis=1, tiled=True),
    )
    all_owner = lax.all_gather(owners[:, 0], "dp", axis=0, tiled=True)
    ordinal = jnp.arange(all_owner.shape[0])
    earlier = (all_owner[None, :] == all_owner[:, None]) & (ordinal[None, :] < ordinal[:, None])
    all_slot = jnp.sum(earlier.astype(jnp.int32), axis=1)
    slot_ids = jnp.arange(CAP)[:, None]
    section_gain = norm_gain[0]
    head_proj = proj_head[0]
    boundary_slab = boundary[0]
    positions = jnp.arange(token_count)
    zero_probe = jnp.zeros((token_count, query_w.shape[1]), jnp.bfloat16)
    tick_count = micro_count + section_count - 1

    def make_layer(seq_length):

        def layer(hidden, probe_in):
            return section_forward(
                hidden, probe_in, query_w, key_w, value_w, out_w, section_gain, seq_length
            )

        return layer

    saved = jnp.zeros_like(boundary_slab)
    incoming = jnp.zeros((token_count, model_width), jnp.bfloat16)
    for moment in range(tick_count):
        micro_index = moment - my_section
        is_live = (micro_index >= 0) & (micro_index < micro_count)
        chosen_micro = jnp.clip(micro_index, 0, micro_count - 1)
        own_slab = lax.dynamic_index_in_dim(boundary_slab, chosen_micro, 0, keepdims=False)
        hidden = jnp.where(my_section == 0, own_slab, incoming)
        current = lax.dynamic_index_in_dim(saved, chosen_micro, 0, keepdims=False)
        saved = lax.dynamic_update_index_in_dim(
            saved, jnp.where(is_live, hidden, current), chosen_micro, 0
        )
        if moment + 1 < tick_count:
            seq_length = lax.dynamic_index_in_dim(lengths, chosen_micro, 0, keepdims=False)
            result, extra = make_layer(seq_length)(hidden, zero_probe)
            incoming = passed_along(result, "section", 1)
    blocks = jnp.zeros((micro_count, 2, proj_rank, proj_rank), jnp.bfloat16)
    incoming = jnp.zeros((token_count, model_width), jnp.bfloat16)
    for moment in range(tick_count):
        micro_index = moment - (section_count - 1 - my_section)
        is_live = (micro_index >= 0) & (micro_index < micro_count)
        chosen_micro = jnp.clip(micro_index, 0, micro_count - 1)
        seq_length = lax.dynamic_index_in_dim(lengths, chosen_micro, 0, keepdims=False)
        valid = positions < seq_length
        own_slab = lax.dynamic_index_in_dim(boundary_slab, chosen_micro, 0, keepdims=False)
        masked_own = jnp.where(valid[:, None], own_slab, jnp.zeros_like(own_slab))
        cotangent = jnp.where(my_section == section_count - 1, masked_own, incoming)
        hidden = lax.dynamic_index_in_dim(saved, chosen_micro, 0, keepdims=False)
        result, pullback, extra = jax.vjp(make_layer(seq_length), hidden, zero_probe, has_aux=True)
        hidden_grad, value_grad = pullback(cotangent)
        new_blocks = module_blocks(
            extra[0], extra[1], value_grad, cotangent, proj_wide, head_proj, valid
        )
        if moment + 1 < tick_count:
            incoming = jax.tree.map(
                lambda part, own: part.astype(own.dtype),
                passed_along(for_sending(hidden_grad), "section", -1),
                hidden_grad,
            )
        current = lax.dynamic_index_in_dim(blocks, chosen_micro, 0, keepdims=False)
        blocks = lax.dynamic_update_index_in_dim(
            blocks, jnp.where(is_live, new_blocks, current), chosen_micro, 0
        )
    piece = lax.all_gather(blocks, "dp", axis=0, tiled=True)
    piece_rows = piece.shape[0]
    picked = ((all_owner[None, :] == my_owner) & (all_slot[None, :] == slot_ids)).astype(
        jnp.bfloat16
    )
    running = jnp.dot(picked, piece.reshape(piece_rows, -1), preferred_element_type=jnp.float32)
    return running.astype(jnp.bfloat16).reshape(CAP, 1, 2, proj_rank, proj_rank)


def solution(mesh):
    return jax.shard_map(
        shards,
        mesh=mesh,
        in_specs=(
            P("section", ("groups", "dp"), None, None),
            P("section", "dp", None),
            P("section", "dp", None),
            P("section", "dp", None),
            P("section", None, "dp"),
            P("section", None),
            P(),
            P("section", None, None, None),
            P(("groups", "dp")),
            P(("groups", "dp"), None),
        ),
        out_specs=P(("groups", "dp"), "section", None, None, None),
        check_vma=False,
    )
```

profile of v0, /device:TPU:0, one launch (start us, length us, event | category | flops | bytes accessed | tf_op | source)
XLA Modules:
  0.0 332.0 jit_solution(5913133050592107326)
XLA Ops:
  6.5 0.7 all-gather.10.cloned.1.call-update
  7.3 0.7 all-gather.12.cloned.1.call-update
  9.3 1.2 dynamic-slice.6
  11.2 0.8 bitcast_dynamic-update-slice_fusion.3
  12.0 13.2 %all-reduce = s32[16]{0:T(128)S(1)} all-reduce(s32[16]{0:T(128)S(1)} %bitcast_dynamic-update-slice_fusion.3), channel_id=2, replica_groups=mesh['groups'=2,'dp'=8,'section'=2] {'dp'}, use_global_device_ids=true, to_apply=%add | all-reduce | flops 16 | bytes 128 | tf_op jit(solution)/shard_map/all_gather | solution.py:96
  25.2 0.8 mul.279
  26.1 1.5 fusion.284
  27.5 1.6 fusion.18
  32.6 1.5 bitcast_dynamic-update-slice_fusion.2
  34.1 27.2 %all-gather.10.cloned.1.call-done = bf16[1,8192,128]{2,1,0:T(8,128)(2,1)} async-done(((bf16[1,1024,128]{2,1,0:T(8,128)(2,1)}), bf16[1,8192,128]{2,1,0:T(8,128)(2,1)}) %all-gather.10.cloned.1.call-update) | async-done | bytes 2097168 | tf_op jit(solution)/shard_map/all_gather | solution.py:91
  61.3 2.5 fusion.84
  63.8 47.3 %all-gather.12.cloned.1.call-done = bf16[1,8192,128]{2,1,0:T(8,128)(2,1)} async-done(((bf16[1,1024,128]{2,1,0:T(8,128)(2,1)}), bf16[1,8192,128]{2,1,0:T(8,128)(2,1)}) %all-gather.12.cloned.1.call-update) | async-done | bytes 2097168 | tf_op jit(solution)/shard_map/all_gather | solution.py:92
  111.1 2.6 fusion.285
  113.7 47.2 %all-gather.14.cloned.1.call-done = bf16[1,8192,128]{2,1,0:T(8,128)(2,1)} async-done(((bf16[1,1024,128]{2,1,0:T(8,128)(2,1)}), bf16[1,8192,128]{2,1,0:T(8,128)(2,1)}) %all-gather.14.cloned.1.call-update) | async-done | bytes 2097168 | tf_op jit(solution)/shard_map/all_gather | solution.py:93
  160.9 2.5 fusion.114
  163.3 47.2 %all-gather.16.cloned.1.call-done = bf16[1,128,8192]{2,1,0:T(8,128)(2,1)} async-done(((bf16[1,128,1024]{2,1,0:T(8,128)(2,1)}), bf16[1,128,8192]{2,1,0:T(8,128)(2,1)}) %all-gather.16.cloned.1.call-update) | async-done | bytes 2097168 | tf_op jit(solution)/shard_map/all_gather | solution.py:94
  210.5 3.6 %fusion = bf16[64,8192]{1,0:T(8,128)(2,1)} fusion(bf16[1,128,8192]{2,1,0:T(8,128)(2,1)} %all-gather.16.cloned.1.call-done, bf16[64,128]{1,0:T(8,128)(2,1)S(1)} %fusion.114, bf16[1,2,64,8192]{3,2,1,0:T(8,128)(2,1)} %param.10, s32[]{:T(128)S(6)} %min.20, pred[]{:T(512)S(6)} %eq.63, f32[64,64]{0,1:T(8,128)S(1)} %get-tuple-element.27, f32[64]{0:T(128)S(1)} %fusion.163, ...), kind=kOutput, calls=%fused_computation.2 | convolution fusion | flops 137383936 | bytes 4227589 | tf_op jit(solution)/shard_map/dot_general | solution.py:49
  214.1 1.5 collective-permute-start
  215.6 1.1 constant_dynamic-slice_fusion.1
  216.8 2.5 fusion.129
  219.8 1.0 copy-done.5
  221.6 2.6 fusion.290
  224.2 2.4 fusion.117
  226.6 3.4 %fusion.1 = bf16[64,8192]{1,0:T(8,128)(2,1)} fusion(bf16[64,8192]{1,0:T(8,128)(2,1)} %copy-done.5, bf16[1,128,8192]{2,1,0:T(8,128)(2,1)} %all-gather.16.cloned.1.call-done, bf16[64,128]{1,0:T(8,128)(2,1)S(1)} %fusion.117, f32[64,64]{0,1:T(8,128)S(1)} %get-tuple-element.29, f32[64]{0:T(128)S(1)} %fusion.164, f32[64]{0:T(128)S(1)} %get-tuple-element.28), kind=kOutput, calls=%fused_computation.3 | convolution fusion | flops 136859648 | bytes 4227584 | tf_op jit(solution)/shard_map/dot_general | solution.py:49
  230.1 1.7 collective-permute-start.1
  231.8 1.8 bitcast_dynamic-update-slice_fusion.1
  237.1 0.7 copy-done.6
  238.8 1.9 fusion.141
  241.5 3.7 %convolution_convert_fusion.3 = bf16[64,8192]{1,0:T(8,128)(2,1)} fusion(bf16[1,8192,128]{2,1,0:T(8,128)(2,1)} %all-gather.10.cloned.1.call-done, bf16[64,128]{1,0:T(8,128)(2,1)S(1)} %fusion.105, f32[64,64]{0,1:T(8,128)S(1)} %get-tuple-element.14, pred[64,64]{0,1:T(32,128)(4,1)S(1)} %get-tuple-element.16, f32[64]{0:T(128)S(1)} %negate_divide_fusion.1, ...), kind=kOutput, calls=%fused_computation.7 | convolution fusion | flops 135823360 | bytes 3182912 | tf_op jit(solution)/shard_map/transpose(jvp())/dot_general | solution.py:33
  245.2 3.6 %convolution_convert_fusion.4 = bf16[64,8192]{1,0:T(8,128)(2,1)} fusion(bf16[1,8192,128]{2,1,0:T(8,128)(2,1)} %all-gather.12.cloned.1.call-done, bf16[64,128]{1,0:T(8,128)(2,1)S(1)} %fusion.90, f32[64,64]{0,1:T(8,128)S(1)} %get-tuple-element.14, pred[64,64]{0,1:T(32,128)(4,1)S(1)} %get-tuple-element.16, f32[64]{0:T(128)S(1)} %negate_divide_fusion.1, ...), kind=kOutput, calls=%fused_computation.8 | convolution fusion | flops 135823360 | bytes 3182912 | tf_op jit(solution)/shard_map/transpose(jvp())/dot_general | solution.py:34
  248.8 3.4 %fusion.24 = (f32[64]{0:T(128)S(1)}, f32[64]{0:T(128)S(1)}, f32[64,8192]{1,0:T(8,128)S(1)}) fusion(bf16[2,64,8192]{2,1,0:T(8,128)(2,1)S(1)} %bitcast_dynamic-update-slice_fusion, s32[]{:T(128)S(6)} %min.19, s32[]{:T(128)S(6)} %min.23, f32[8192]{0:T(1024)S(1)} %bitcast.284, bf16[64,8192]{1,0:T(8,128)(2,1)} %convolution_convert_fusion.3, ...), kind=kOutput, calls=%fused_computation.49 | convolution fusion | flops 139984768 | bytes 8438280 | tf_op jit(solution)/shard_map/transpose(jvp())/dot_general | solution.py:36
  252.2 1.8 fusion.16
  254.0 1.4 collective-permute-start.2
  256.8 0.9 copy-done.7
  259.1 2.8 fusion.153
  261.8 1.8 fusion.143
  263.6 2.8 fusion.132
  266.9 3.6 %convolution_convert_fusion = bf16[64,8192]{1,0:T(8,128)(2,1)} fusion(bf16[1,8192,128]{2,1,0:T(8,128)(2,1)} %all-gather.10.cloned.1.call-done, bf16[64,128]{1,0:T(8,128)(2,1)S(1)} %fusion.108, f32[64,64]{0,1:T(8,128)S(1)} %get-tuple-element.10, pred[64,64]{0,1:T(32,128)(4,1)S(1)} %get-tuple-element.12, f32[64]{0:T(128)S(1)} %negate_divide_fusion, ...), kind=kOutput, calls=%fused_computation.4 | convolution fusion | flops 135823360 | bytes 3182912 | tf_op jit(solution)/shard_map/transpose(jvp())/dot_general | solution.py:33
  270.5 3.6 %convolution_convert_fusion.1 = bf16[64,8192]{1,0:T(8,128)(2,1)} fusion(bf16[1,8192,128]{2,1,0:T(8,128)(2,1)} %all-gather.12.cloned.1.call-done, bf16[64,128]{1,0:T(8,128)(2,1)S(1)} %fusion.93, f32[64,64]{0,1:T(8,128)S(1)} %get-tuple-element.10, pred[64,64]{0,1:T(32,128)(4,1)S(1)} %get-tuple-element.12, f32[64]{0:T(128)S(1)} %negate_divide_fusion, ...), kind=kOutput, calls=%fused_computation.5 | convolution fusion | flops 135823360 | bytes 3182912 | tf_op jit(solution)/shard_map/transpose(jvp())/dot_general | solution.py:34
  274.1 3.3 fusion.28
  277.4 1.6 fusion.17
  279.0 1.5 collective-permute-start.3
  281.7 2.2 fusion.297
  284.0 2.1 fusion.126
  286.4 3.1 fusion.135
  290.4 2.2 fusion.145
  292.7 31.4 %all_gather.23 = bf16[16,2,64,64]{3,2,1,0:T(8,128)(2,1)S(1)} all-gather(bf16[2,2,64,64]{3,2,1,0:T(8,128)(2,1)S(1)} %fusion.157), channel_id=1, replica_groups=mesh['groups'=2,'dp'=8,'section'=2] {'dp'}, dimensions={0}, use_global_device_ids=true | all-gather | bytes 294912 | tf_op jit(solution)/shard_map/all_gather | solution.py:160
  324.7 0.8 reshape.291
  (99 shorter events, 17.7 us)
Async XLA Ops:
  6.5 232.2 %copy-start = (bf16[64,8192]{1,0:T(8,128)(2,1)S(1)}, bf16[64,8192]{1,0:T(8,128)(2,1)}, u32[]{:S(2)}) copy-start(bf16[64,8192]{1,0:T(8,128)(2,1)} %param.16) | copy-start | bytes 3145732
  6.5 54.8 %all-gather.10.cloned.1.call-start = ((), (), s32[]{:S(2)}) async-start(), calls=%async_computation | async-start | bytes 2359296 | tf_op jit(solution)/shard_map/all_gather | solution.py:91
  7.3 103.8 %all-gather.12.cloned.1.call-start = ((), (), s32[]{:S(2)}) async-start(), calls=%async_computation.1 | async-start | bytes 2359296 | tf_op jit(solution)/shard_map/all_gather | solution.py:92
  8.0 152.9 %all-gather.14.cloned.1.call-start = ((), (), s32[]{:S(2)}) async-start(), calls=%async_computation.2 | async-start | bytes 2359296 | tf_op jit(solution)/shard_map/all_gather | solution.py:93
  8.7 201.8 %all-gather.16.cloned.1.call-start = ((), (), s32[]{:S(2)}) async-start(), calls=%async_computation.3 | async-start | bytes 2359296 | tf_op jit(solution)/shard_map/all_gather | solution.py:94
  214.1 2.6 copy-start.1
  214.1 5.1 %collective-permute-start = (bf16[64,8192]{1,0:T(8,128)(2,1)}, bf16[64,8192]{1,0:T(8,128)(2,1)S(1)}, u32[]{:S(2)}, u32[]{:S(2)}) collective-permute-start(bf16[64,8192]{1,0:T(8,128)(2,1)} %fusion), channel_id=1, source_target_pairs={{0,1},{2,3},{4,5},{6,7},{8,9},{10,11},{12,13},{14,15},{16,17},{18,... | collective-permute-start | bytes 3145736 | tf_op jit(solution)/shard_map/ppermute | solution.py:16
  219.2 1.9 copy-start.10
  219.7 1.0 copy-start.5
  230.1 3.9 %copy-start.2 = (bf16[1,2,64,8192]{3,2,1,0:T(8,128)(2,1)S(1)}, bf16[1,2,64,8192]{3,2,1,0:T(8,128)(2,1)}, u32[]{:S(2)}) copy-start(bf16[1,2,64,8192]{3,2,1,0:T(8,128)(2,1)} %param.10) | copy-start | bytes 6291460
  230.1 3.9 %collective-permute-start.1 = (bf16[64,8192]{1,0:T(8,128)(2,1)}, bf16[64,8192]{1,0:T(8,128)(2,1)S(1)}, u32[]{:S(2)}, u32[]{:S(2)}) collective-permute-start(bf16[64,8192]{1,0:T(8,128)(2,1)} %fusion.1), channel_id=1, source_target_pairs={{0,1},{2,3},{4,5},{6,7},{8,9},{10,11},{12,13},{14,15},{16,17},{18,... | collective-permute-start | bytes 3145736 | tf_op jit(solution)/shard_map/ppermute | solution.py:16
  233.7 1.6 copy-start.11
  234.5 1.7 copy-start.8
  236.2 1.6 copy-start.6
  236.7 1.6 copy-start.14
  248.8 3.4 %copy-start.3 = (bf16[1,2,64,8192]{3,2,1,0:T(8,128)(2,1)S(1)}, bf16[1,2,64,8192]{3,2,1,0:T(8,128)(2,1)}, u32[]{:S(2)}) copy-start(bf16[1,2,64,8192]{3,2,1,0:T(8,128)(2,1)} %param.10) | copy-start | bytes 6291460
  252.2 3.3 copy-start.12
  254.0 2.0 copy-start.9
  254.0 5.0 %collective-permute-start.2 = (bf16[64,8192]{1,0:T(8,128)(2,1)}, bf16[64,8192]{1,0:T(8,128)(2,1)}, u32[]{:S(2)}, u32[]{:S(2)}) collective-permute-start(bf16[64,8192]{1,0:T(8,128)(2,1)} %fusion.16), channel_id=1, source_target_pairs={{1,0},{3,2},{5,4},{7,6},{9,8},{11,10},{13,12},{15,14},{17,16},{19,... | collective-permute-start | bytes 3145736 | tf_op jit(solution)/shard_map/ppermute | solution.py:16
  256.1 1.6 copy-start.7
  274.1 3.3 %copy-start.4 = (bf16[64,8192]{1,0:T(8,128)(2,1)S(1)}, bf16[64,8192]{1,0:T(8,128)(2,1)}, u32[]{:S(2)}) copy-start(bf16[64,8192]{1,0:T(8,128)(2,1)} %fusion.153) | copy-start | bytes 3145732
  277.4 3.1 copy-start.13
  279.0 7.4 %collective-permute-start.3 = (bf16[64,8192]{1,0:T(8,128)(2,1)}, bf16[64,8192]{1,0:T(8,128)(2,1)}, u32[]{:S(2)}, u32[]{:S(2)}) collective-permute-start(bf16[64,8192]{1,0:T(8,128)(2,1)} %fusion.17), channel_id=1, source_target_pairs={{1,0},{3,2},{5,4},{7,6},{9,8},{11,10},{13,12},{15,14},{17,16},{19,... | collective-permute-start | bytes 3145736 | tf_op jit(solution)/shard_map/ppermute | solution.py:16
Sparse Core Ops, SparseCore 0:
  9.5 51.8 all-gather.9
  63.4 47.6 all-gather.11
  113.2 47.6 all-gather.13
  162.9 47.5 all-gather.15
where the time goes:
time: 333 us; the launch traced here: 332 us
  waiting for transfers between devices  172 us (52%)
  matrix products  67.7 us (20%)
  blocking collectives  44.6 us (13%)
  other arithmetic  16.9 us (5%)
  between operations  14.3 us (4%)
  local copies, waits for them, and re-layouts  10 us (3%)
  starting transfers between devices  6.16 us (2%)
    all_gather x1, waiting for transfers between devices, shards(): lax.all_gather(w_key[0], 'dp', axis=0, tiled=True)  47.3 us
    all_gather x1, waiting for transfers between devices, shards(): lax.all_gather(w_out[0], 'dp', axis=1, tiled=True)  47.2 us
    all_gather x1, waiting for transfers between devices, shards(): lax.all_gather(w_value[0], 'dp', axis=0, tiled=True)  47.2 us
    all_gather x1, blocking collectives, shards(): piece = lax.all_gather(blocks, 'dp', axis=0, tiled=True)  31.4 us
    all_gather x1, waiting for transfers between devices, shards(): lax.all_gather(w_query[0], 'dp', axis=0, tiled=True)  27.2 us
    dot_general x5, matrix products, section_forward(): jnp.dot(mixed, w_out, preferred_element_type=jnp.float32)  15.4 us
    dot_general x7, matrix products, section_forward(): jnp.dot(normed, w_value, preferred_element_type=jnp.float32)  14.6 us
    all_gather x1, blocking collectives, shards(): all_owner = lax.all_gather(owners[:, 0], 'dp', axis=0, tiled=True)  13.2 us
  transfers between devices with their start and end apart: 8, of which 6 were waited for; matrix products, arithmetic and copies ran while one was open for 10% of the time, Pallas kernels for 0%

commit v1 on v0

v1 whole, which is shorter than its diff:
```python
import functools

import jax
import jax.numpy as jnp
from jax import lax
from jax.experimental import pallas as pl
from jax.experimental.pallas import tpu as pltpu
from jax.sharding import PartitionSpec as P

CAP = 4
EPSILON = 1e-05
MASKED = -1e30
MESH = pl.DeviceIdType.MESH
F32 = jnp.float32
BF16 = jnp.bfloat16


def nn(a, b):
    return lax.dot_general(a, b, (((1,), (0,)), ((), ())), preferred_element_type=F32)


def nt(a, b):
    return lax.dot_general(a, b, (((1,), (1,)), ((), ())), preferred_element_type=F32)


def tn(a, b):
    return lax.dot_general(a, b, (((0,), (0,)), ((), ())), preferred_element_type=F32)


def kernel(
    n, examples, length, chunk,
    len_ref, w_ref, x_ref, gain_ref, wide_ref, head_ref, own_ref,
    out_ref,
    g_ref, wo_ref, far_ref, norm_ref, mid_ref, acc_ref, pin_ref, prb_ref,
    mix_ref, back_ref, mixin_ref, backin_ref, blk_ref, all_ref, own_all, pick_ref,
    loc_sem, send_sem, cw_sem, ccw_sem, y_sem, wo_send, wo_recv,
    x_send, x_recv, mix_send, mix_recv, back_send, back_recv,
    own_send, own_recv, blk_send, blk_recv,
):
    group = lax.axis_index("groups")
    me = lax.axis_index("dp")
    sec = lax.axis_index("section")
    rows = w_ref.shape[0]
    tokens, width = x_ref.shape
    hd = wo_ref.shape[1]
    rank = wide_ref.shape[0]
    third = rows // 3 // 16 * 16
    mid = rows - 2 * third
    mine = group * (rows - third)
    theirs = (1 - group) * (rows - third)
    half = n // 2
    parity = me % 2
    place = me // 2 + parity * (n - 1 - 2 * (me // 2))

    def at(position):
        position = (position + 2 * n) % n
        high = position // half
        return (1 - high) * 2 * position + high * (2 * (n - 1 - position) + 1)

    nxt, prv = at(place + 1), at(place - 1)

    barrier = pltpu.get_barrier_semaphore()

    def greet(i, carry):
        pl.semaphore_signal(
            barrier, inc=1, device_id={"dp": (me + i) % n}, device_id_type=MESH
        )
        return carry

    own_block = pltpu.make_async_copy(w_ref, g_ref.at[pl.ds(me * rows, rows)], loc_sem)
    own_block.start()
    lax.fori_loop(1, n, greet, 0)
    pl.semaphore_signal(barrier, inc=1, device_id={"groups": 1 - group}, device_id_type=MESH)
    pl.semaphore_signal(barrier, inc=1, device_id={"section": 1 - sec}, device_id_type=MESH)
    own_block.wait()
    pl.semaphore_wait(barrier, n + 1)

    def part(origin, offset, size):
        return g_ref.at[pl.ds(pl.multiple_of(origin * rows + offset, 16), size)]

    def hop(ref, sem, target):
        return pltpu.make_async_remote_copy(
            src_ref=ref, dst_ref=ref, send_sem=send_sem, recv_sem=sem,
            device_id=target, device_id_type=MESH,
        )

    def cw(s, origin):
        return hop(part(at(origin), mine, third), cw_sem.at[s], {"dp": nxt})

    def ccw(s, origin):
        return hop(part(at(origin), third, mid), ccw_sem.at[s], {"dp": prv})

    def over(s, origin, offset):
        return hop(part(at(origin), offset, third), y_sem.at[s], {"groups": 1 - group})

    def hand_over(origin, offset, size):
        start = pl.multiple_of(at(origin) * rows + offset, 16)

        @pl.when(sec == 0)
        def _():
            pltpu.make_async_remote_copy(
                src_ref=g_ref.at[pl.ds(start, size), pl.ds(3 * hd, hd)],
                dst_ref=wo_ref.at[pl.ds(start, size)],
                send_sem=wo_send, recv_sem=wo_recv,
                device_id={"section": 1 - sec}, device_id_type=MESH,
            ).start()

    def across(src, dst, send, recv):
        return pltpu.make_async_remote_copy(
            src_ref=src, dst_ref=dst, send_sem=send, recv_sem=recv,
            device_id={"section": 1 - sec}, device_id_type=MESH,
        )

    cw(0, place).start()
    ccw(0, place).start()
    give_x = across(x_ref, far_ref, x_send, x_recv)

    @pl.when(sec == 0)
    def _():
        give_x.start()

    hand_over(place, 0, rows)

    def tell(i, carry):
        pltpu.make_async_remote_copy(
            src_ref=own_ref, dst_ref=own_all.at[me], send_sem=own_send, recv_sem=own_recv,
            device_id={"dp": (me + i) % n}, device_id_type=MESH,
        ).start()
        return carry

    lax.fori_loop(1, n, tell, 0)
    own_all[me] = own_ref[...]

    row = lax.broadcasted_iota(jnp.int32, (tokens, 1), 0)
    reach = jnp.zeros((tokens, 1), jnp.int32)
    for e in range(examples):
        reach = jnp.where(row // length == e, len_ref[e] + e * length, reach)
    valid = row < reach
    row2 = lax.broadcasted_iota(jnp.int32, (tokens, tokens), 0)
    col2 = lax.broadcasted_iota(jnp.int32, (tokens, tokens), 1)
    allowed = (col2 <= row2) & (col2 < reach) & (row2 // length == col2 // length)
    scale = hd ** (-0.5)
    chunks = width // chunk

    def cols(c):
        return pl.ds(pl.multiple_of(c * chunk, chunk), chunk)

    def rms(ref):
        def add(c, total):
            value = ref[:, cols(c)].astype(F32)
            return total + jnp.sum(value * value, axis=1, keepdims=True)

        total = lax.fori_loop(0, chunks, add, jnp.zeros((tokens, 1), F32))
        return lax.rsqrt(total / width + EPSILON)

    def normalise(ref, inverse):
        def one(c, carry):
            value = ref[:, cols(c)].astype(F32) * inverse * gain_ref[:, cols(c)].astype(F32)
            value = value.astype(BF16)
            norm_ref[:, cols(c)] = value
            pin_ref[...] += nt(value, wide_ref[:, cols(c)])
            return carry

        lax.fori_loop(0, chunks, one, 0)

    def projections():
        acc_ref[...] = jnp.zeros_like(acc_ref)

        def one(c, carry):
            acc_ref[...] += nn(norm_ref[:, cols(c)], g_ref[cols(c), pl.ds(0, 3 * hd)])
            return carry

        lax.fori_loop(0, chunks, one, 0)

    def attention():
        q = acc_ref[:, 0:hd].astype(BF16)
        k = acc_ref[:, hd : 2 * hd].astype(BF16)
        v = acc_ref[:, 2 * hd : 3 * hd].astype(BF16)
        scores = jnp.where(allowed, nt(q, k) * scale, MASKED)
        raised = jnp.exp(scores - jnp.max(scores, axis=1, keepdims=True))
        probs = raised / jnp.sum(raised, axis=1, keepdims=True)
        mixed = nn(probs.astype(BF16), v).astype(BF16)
        return q, k, v, probs, mixed

    def finish(mixed, dvalue, wide_out):
        head_in = nt(mixed, head_ref[1]).astype(BF16)
        value_side = jnp.where(valid, nt(dvalue, head_ref[0]), 0.0).astype(BF16)
        wide_in = pin_ref[...].astype(BF16)
        for e in range(examples):
            span = slice(e * length, (e + 1) * length)
            first = tn(value_side[span], wide_in[span])
            second = tn(wide_out[span], head_in[span])
            blk_ref[e] = jnp.concatenate([first, second], axis=1).astype(BF16)

    pin_ref[...] = jnp.zeros_like(pin_ref)

    @pl.when(sec == 0)
    def _():
        normalise(x_ref, rms(x_ref))

    def step(s, carry):
        cw(s - 1, place - s).wait_recv()
        cw(s, place - s).start()
        over(s, place - s, mine).start()
        hand_over(place - s, mine, third)
        ccw(s - 1, place + s).wait_recv()
        ccw(s, place + s).start()
        hand_over(place + s, third, mid)
        return carry

    lax.fori_loop(1, n - 1, step, 0)
    cw(n - 2, place - (n - 1)).wait_recv()
    over(n - 1, place - (n - 1), mine).start()
    hand_over(place - (n - 1), mine, third)
    ccw(n - 2, place + n - 1).wait_recv()
    hand_over(place + n - 1, third, mid)

    def take(s, carry):
        over(s, place - s, theirs).wait_recv()
        hand_over(place - s, theirs, third)
        return carry

    lax.fori_loop(1, n, take, 0)

    give_mix = across(mix_ref, mixin_ref, mix_send, mix_recv)
    give_back = across(back_ref, backin_ref, back_send, back_recv)
    give_wo = across(wo_ref, wo_ref, wo_send, wo_recv)

    @pl.when(sec == 0)
    def _():
        projections()
        _, _, _, probs, mixed = attention()
        mix_ref[...] = mixed
        give_mix.start()
        prb_ref[...] = probs.astype(BF16)
        give_back.wait_recv()
        dmixed = backin_ref[:, 0:hd]
        wide_out = backin_ref[:, hd : hd + rank]
        dvalue = tn(prb_ref[...], dmixed).astype(BF16)
        finish(mix_ref[...], dvalue, wide_out)
        give_mix.wait_send()
        give_x.wait_send()
        give_wo.wait_send()

    @pl.when(sec == 1)
    def _():
        acc_ref[...] = jnp.zeros_like(acc_ref)

        def early(c, carry):
            cot = jnp.where(valid, x_ref[:, cols(c)].astype(F32), 0.0).astype(BF16)
            acc_ref[:, 0:hd] += nn(cot, g_ref[cols(c), pl.ds(3 * hd, hd)])
            acc_ref[:, hd : hd + rank] += nt(cot, wide_ref[:, cols(c)])
            return carry

        lax.fori_loop(0, chunks, early, 0)
        dmixed = acc_ref[:, 0:hd].astype(BF16)
        wide_out = acc_ref[:, hd : hd + rank].astype(BF16)
        give_x.wait_recv()
        give_wo.wait_recv()
        give_mix.wait_recv()
        before = mixin_ref[...]

        def advance(c, total):
            value = far_ref[:, cols(c)].astype(F32) + nt(before, wo_ref[cols(c), :])
            value = value.astype(BF16)
            mid_ref[:, cols(c)] = value
            value = value.astype(F32)
            return total + jnp.sum(value * value, axis=1, keepdims=True)

        total = lax.fori_loop(0, chunks, advance, jnp.zeros((tokens, 1), F32))
        inverse = lax.rsqrt(total / width + EPSILON)
        normalise(mid_ref, inverse)
        projections()
        q, k, v, probs, mixed = attention()
        rounded = probs.astype(BF16)
        dvalue = tn(rounded, dmixed).astype(BF16)
        dprobs = nt(dmixed, v)
        inner = jnp.sum(dprobs * probs, axis=1, keepdims=True)
        dscores = (probs * (dprobs - inner) * scale).astype(BF16)
        dq = nn(dscores, k).astype(BF16)
        dk = tn(dscores, q).astype(BF16)
        dall = jnp.concatenate([dq, dk, dvalue], axis=1)
        share = jnp.sum(dall.astype(F32) * acc_ref[...], axis=1, keepdims=True)
        share = share * inverse * inverse / width
        acc_ref[...] = jnp.zeros_like(acc_ref)

        def retreat(c, carry):
            dnorm = nt(dall, g_ref[cols(c), pl.ds(0, 3 * hd)])
            cot = jnp.where(valid, x_ref[:, cols(c)].astype(F32), 0.0)
            cot = cot + dnorm * inverse * gain_ref[:, cols(c)].astype(F32)
            cot = (cot - mid_ref[:, cols(c)].astype(F32) * share).astype(BF16)
            acc_ref[:, 0:hd] += nn(cot, wo_ref[cols(c), :])
            acc_ref[:, hd : hd + rank] += nt(cot, wide_ref[:, cols(c)])
            return carry

        lax.fori_loop(0, chunks, retreat, 0)
        back_ref[:, 0:hd] = acc_ref[:, 0:hd].astype(BF16)
        back_ref[:, hd : 2 * hd] = jnp.where(valid, acc_ref[:, hd : 2 * hd], 0.0).astype(BF16)
        give_back.start()
        finish(mixed, dvalue, wide_out)
        give_back.wait_send()

    def spread(i, carry):
        pltpu.make_async_remote_copy(
            src_ref=blk_ref, dst_ref=all_ref.at[me], send_sem=blk_send, recv_sem=blk_recv,
            device_id={"dp": (me + i) % n}, device_id_type=MESH,
        ).start()
        return carry

    lax.fori_loop(1, n, spread, 0)
    all_ref[me] = blk_ref[...]

    def everyone(ref, send, recv):
        return pltpu.make_async_remote_copy(
            src_ref=ref.at[pl.ds(0, n - 1)], dst_ref=ref.at[pl.ds(0, n - 1)],
            send_sem=send, recv_sem=recv, device_id={"dp": nxt}, device_id_type=MESH,
        )

    told = everyone(own_all, own_send, own_recv)
    told.wait_recv()
    pick_ref[...] = jnp.zeros_like(pick_ref)
    shared = everyone(all_ref, blk_send, blk_recv)
    shared.wait_recv()

    def choose(i, seen):
        for e in range(examples):
            named = jnp.where(own_all[i, pl.ds(e, 1), :] == me, 1.0, 0.0)
            piece = all_ref[i, e].astype(F32)
            for slot in range(CAP):
                weight = jnp.where(seen == float(slot), named, 0.0)
                pick_ref[slot] += weight * piece
            seen = seen + named
        return seen

    lax.fori_loop(0, n, choose, jnp.zeros((1, 2 * rank), F32))
    for slot in range(CAP):
        out_ref[slot, 0] = pick_ref[slot, :, 0:rank].astype(BF16)
        out_ref[slot, 1] = pick_ref[slot, :, rank : 2 * rank].astype(BF16)

    told.wait_send()
    shared.wait_send()

    def drain(s, carry):
        cw(s, place).wait_send()
        ccw(s, place).wait_send()
        over(s + 1, place, mine).wait_send()
        return carry

    lax.fori_loop(0, n - 1, drain, 0)


def shards(
    boundary, w_query, w_key, w_value, w_out, norm_gain, proj_wide, proj_head, lengths, owners
):
    n = lax.axis_size("dp")
    examples, length, width = boundary.shape[1:]
    rows, hd = w_query.shape[1:]
    rank = proj_wide.shape[0]
    tokens = examples * length
    chunk = min(width, 1024)
    weights = jnp.concatenate([w_query[0], w_key[0], w_value[0], w_out[0].T], axis=1)
    padded = -(-examples // 8) * 8
    own = jnp.pad(owners, ((0, padded - examples), (0, 0)))
    own = jnp.broadcast_to(own, (padded, 2 * rank))
    vmem = pl.BlockSpec(memory_space=pltpu.VMEM)
    dma = pltpu.SemaphoreType.DMA
    out = pl.pallas_call(
        functools.partial(kernel, n, examples, length, chunk),
        out_shape=jax.ShapeDtypeStruct((CAP, 2, rank, rank), BF16),
        in_specs=[
            pl.BlockSpec(memory_space=pltpu.SMEM), pl.BlockSpec(memory_space=pl.ANY),
            vmem, vmem, vmem, vmem, vmem,
        ],
        out_specs=vmem,
        scratch_shapes=[
            pltpu.VMEM((width, 4 * hd), BF16),
            pltpu.VMEM((width, hd), BF16),
            pltpu.VMEM((tokens, width), BF16),
            pltpu.VMEM((tokens, width), BF16),
            pltpu.VMEM((tokens, width), BF16),
            pltpu.VMEM((tokens, 3 * hd), F32),
            pltpu.VMEM((tokens, rank), F32),
            pltpu.VMEM((tokens, tokens), BF16),
            pltpu.VMEM((tokens, hd), BF16),
            pltpu.VMEM((tokens, 2 * hd), BF16),
            pltpu.VMEM((tokens, hd), BF16),
            pltpu.VMEM((tokens, 2 * hd), BF16),
            pltpu.VMEM((examples, rank, 2 * rank), BF16),
            pltpu.VMEM((n, examples, rank, 2 * rank), BF16),
            pltpu.VMEM((n, padded, 2 * rank), jnp.int32),
            pltpu.VMEM((CAP, rank, 2 * rank), F32),
            dma, dma, dma((n,)), dma((n,)), dma((n,)), dma, dma,
            dma, dma, dma, dma, dma, dma,
            dma, dma, dma, dma,
        ],
        compiler_params=pltpu.CompilerParams(
            collective_id=0, has_side_effects=True, vmem_limit_bytes=56 * 1024 * 1024
        ),
    )(
        lengths, weights, boundary.reshape(tokens, width), norm_gain,
        proj_wide, proj_head[0], own,
    )
    return out[:, None]


def solution(mesh):
    return jax.shard_map(
        shards,
        mesh=mesh,
        in_specs=(
            P("section", ("groups", "dp"), None, None),
            P("section", "dp", None),
            P("section", "dp", None),
            P("section", "dp", None),
            P("section", None, "dp"),
            P("section", None),
            P(),
            P("section", None, None, None),
            P(("groups", "dp")),
            P(("groups", "dp"), None),
        ),
        out_specs=P(("groups", "dp"), "section", None, None, None),
        check_vma=False,
    )
```

time: 333 us -> 102 us (0.31)
  waiting for transfers between devices: 172 us -> 0 us
  Pallas kernels: 0 us -> 96.3 us
  matrix products: 67.7 us -> 0 us
  blocking collectives: 44.6 us -> 0 us
  other arithmetic: 16.9 us -> 2.21 us
  between operations: 14.3 us -> 0.02 us
  local copies, waits for them, and re-layouts: 10 us -> 3.37 us
  starting transfers between devices: 6.16 us -> 0 us
    all_gather x4 -> x0, waiting for transfers between devices: 169 us -> none  [the longest x1 47.3 us: shards(): lax.all_gather(w_key[0], 'dp', axis=0, tiled=True)]
    pallas_call x0 -> x1, Pallas kernels: none -> 96.3 us  [shards(): pl.pallas_call(functools.partial(kernel, n, examples, length, chunk), out...]
    dot_general x45 -> x0, matrix products: 67.7 us -> none  [the longest x5 15.4 us: section_forward(): jnp.dot(mixed, w_out, preferred_element_type=jnp.float32)]
    all_gather x2 -> x0, blocking collectives: 44.6 us -> none  [the longest x1 31.4 us: shards(): piece = lax.all_gather(blocks, 'dp', axis=0, tiled=True)]
    ppermute x4 -> x0, starting transfers between devices: 6.04 us -> none  [passed_along(): return lax.ppermute(array, axis, pairs)]
    dynamic_update_slice x6 -> x0, other arithmetic: 3.93 us -> none  [the longest x3 3.84 us: shards(): lax.dynamic_update_index_in_dim(saved, jnp.where(is_live, hidden, current...]
    convert_element_type x2 -> x0, other arithmetic: 3.39 us -> none  [section_forward(): widened = hidden.astype(jnp.float32)]
  transfers between devices with their start and end apart: 8 -> 0, of which waited for: 6 -> 0; matrix products, arithmetic and copies ran while one was open for 10% -> 0% of each run, Pallas kernels for 0% -> 0%
where the time goes in v1:
time: 102 us
  Pallas kernels  96.3 us (94%)
  local copies, waits for them, and re-layouts  3.37 us (3%)
  other arithmetic  2.21 us (2%)
    pallas_call x1, Pallas kernels, shards(): pl.pallas_call(functools.partial(kernel, n, examples, length, chunk), out...  96.3 us
    unnamed x4, local copies, waits for them, and re-layouts  2.7 us
    concatenate x1, other arithmetic, shards(): jnp.concatenate([w_query[0], w_key[0], w_value[0], w_out[0].T], axis=1)  2.21 us

profile of v1, /device:TPU:0, one launch (start us, length us, event | category | flops | bytes accessed | tf_op | source)
XLA Modules:
  0.0 101.9 jit_solution(2289855052681555748)
XLA Ops:
  0.0 0.0 copy-start
  0.0 1.1 %copy.11 = bf16[1,128,1024]{1,2,0:T(8,128)(2,1)S(1)} copy(bf16[1,128,1024]{2,1,0:T(8,128)(2,1)} %param.14) | data formatting | bytes 524288 | tf_op args[4]
  1.1 2.2 %pad_maximum_fusion.w_ref = bf16[1024,512]{1,0:T(8,128)(2,1)} fusion(bf16[1024,128]{1,0:T(8,128)(2,1)S(1)} %bitcast.14, bf16[1024,128]{1,0:T(8,128)(2,1)} %bitcast.16, bf16[1024,128]{1,0:T(8,128)(2,1)} %bitcast.17, bf16[1024,128]{1,0:T(8,128)(2,1)} %bitcast.18), kind=kLoop, calls=%fused_computation | loop fusion | flops 4194304 | bytes 2097152 | tf_op jit(solution)/shard_map/concatenate | solution.py:361
  3.4 0.0 copy-done
  3.4 0.7 broadcast_in_dim.11.own_ref
  4.0 96.3 %shard_map.100 = bf16[4,2,64,64]{3,2,1,0:T(8,128)(2,1)} custom-call(s32[2]{0:T(128)} %len_ref.1, bf16[1024,512]{1,0:T(8,128)(2,1)} %pad_maximum_fusion.w_ref, bf16[128,8192]{1,0:T(8,128)(2,1)} %bitcast.13, bf16[1,8192]{1,0:T(2,128)(2,1)} %gain_ref.1, bf16[64,8192]{1,0:T(8,128)(2,1)} %wide_ref.1, bf16[2,64,128]{2,1,0:T(8,128)(2,1)} %bitcast.19, ...), custom_call_target="tpu_custom_call" | custom-call | tf_op jit(solution)/shard_map/pallas_call | solution.py:367
  100.3 1.6 %copy.14 = bf16[4,1,2,64,64]{4,3,2,1,0:T(8,128)(2,1)} copy(bf16[4,1,2,64,64]{4,3,2,1,0:T(8,128)(2,1)} %bitcast.15) | data formatting | bytes 131072
  (1 shorter events, 0.0 us)
Async XLA Ops:
  0.0 3.4 %copy-start = (s32[2,1]{0,1:T(1,128)S(1)}, s32[2,1]{0,1:T(1,128)}, u32[]{:S(2)}) copy-start(s32[2,1]{0,1:T(1,128)} %param.19) | copy-start | bytes 28

commit v2 on v1

--- a/solution.py
+++ b/solution.py
@@ -28,11 +28,12 @@
 
 
 def kernel(
-    n, examples, length, chunk,
+    n, examples, length, parts,
     len_ref, w_ref, x_ref, gain_ref, wide_ref, head_ref, own_ref,
     out_ref,
-    g_ref, wo_ref, far_ref, norm_ref, mid_ref, acc_ref, pin_ref, prb_ref,
-    mix_ref, back_ref, mixin_ref, backin_ref, blk_ref, all_ref, own_all, pick_ref,
+    g_ref, wo_ref, left_ref, accl_ref, accm_ref, accc_ref, pre_ref, acc_ref, sq_ref,
+    pin_ref, prb_ref, mix_ref, back_ref, mixin_ref, backin_ref, blk_ref, all_ref,
+    own_all, pick_ref,
     loc_sem, send_sem, cw_sem, ccw_sem, y_sem, wo_send, wo_recv,
     x_send, x_recv, mix_send, mix_recv, back_send, back_recv,
     own_send, own_recv, blk_send, blk_recv,
@@ -52,6 +53,14 @@
     parity = me % 2
     place = me // 2 + parity * (n - 1 - 2 * (me // 2))
 
+    def pieces(size):
+        if parts == 1:
+            return ((0, size),)
+        first = (size // 2 + 15) // 16 * 16
+        return ((0, first), (first, size - first))
+
+    side, middle = pieces(third), pieces(mid)
+
     def at(position):
         position = (position + 2 * n) % n
         high = position // half
@@ -84,24 +93,32 @@
             device_id=target, device_id_type=MESH,
         )
 
-    def cw(s, origin):
-        return hop(part(at(origin), mine, third), cw_sem.at[s], {"dp": nxt})
-
-    def ccw(s, origin):
-        return hop(part(at(origin), third, mid), ccw_sem.at[s], {"dp": prv})
-
-    def over(s, origin, offset):
-        return hop(part(at(origin), offset, third), y_sem.at[s], {"groups": 1 - group})
-
-    def hand_over(origin, offset, size):
-        start = pl.multiple_of(at(origin) * rows + offset, 16)
+    def cw(s, j, origin):
+        offset, size = side[j]
+        return hop(part(at(origin), mine + offset, size), cw_sem.at[s * parts + j], {"dp": nxt})
+
+    def ccw(s, j, origin):
+        offset, size = middle[j]
+        return hop(
+            part(at(origin), third + offset, size), ccw_sem.at[s * parts + j], {"dp": prv}
+        )
+
+    def over(s, j, origin, base):
+        offset, size = side[j]
+        return hop(
+            part(at(origin), base + offset, size),
+            y_sem.at[s * parts + j], {"groups": 1 - group},
+        )
+
+    def hand_over(index, offset, size):
+        start = pl.multiple_of(at(place - index) * rows + offset, 16)
 
         @pl.when(sec == 0)
         def _():
             pltpu.make_async_remote_copy(
                 src_ref=g_ref.at[pl.ds(start, size), pl.ds(3 * hd, hd)],
                 dst_ref=wo_ref.at[pl.ds(start, size)],
-                send_sem=wo_send, recv_sem=wo_recv,
+                send_sem=wo_send, recv_sem=wo_recv.at[index],
                 device_id={"section": 1 - sec}, device_id_type=MESH,
             ).start()
 
@@ -111,15 +128,16 @@
             device_id={"section": 1 - sec}, device_id_type=MESH,
         )
 
-    cw(0, place).start()
-    ccw(0, place).start()
-    give_x = across(x_ref, far_ref, x_send, x_recv)
+    for j in range(parts):
+        cw(0, j, place).start()
+        ccw(0, j, place).start()
+    give_x = across(x_ref, left_ref.at[pl.ds(0, tokens)], x_send, x_recv)
 
     @pl.when(sec == 0)
     def _():
         give_x.start()
 
-    hand_over(place, 0, rows)
+    hand_over(0, 0, rows)
 
     def tell(i, carry):
         pltpu.make_async_remote_copy(
@@ -140,37 +158,154 @@
     col2 = lax.broadcasted_iota(jnp.int32, (tokens, tokens), 1)
     allowed = (col2 <= row2) & (col2 < reach) & (row2 // length == col2 // length)
     scale = hd ** (-0.5)
+    chunk = min(width, 1024)
     chunks = width // chunk
+    by_block = rows % 128 == 0
+    t1, t2, t3, t4 = tokens, 2 * tokens, 2 * tokens + rank, 2 * tokens + 2 * rank
 
     def cols(c):
         return pl.ds(pl.multiple_of(c * chunk, chunk), chunk)
 
-    def rms(ref):
-        def add(c, total):
-            value = ref[:, cols(c)].astype(F32)
-            return total + jnp.sum(value * value, axis=1, keepdims=True)
-
-        total = lax.fori_loop(0, chunks, add, jnp.zeros((tokens, 1), F32))
-        return lax.rsqrt(total / width + EPSILON)
-
-    def normalise(ref, inverse):
+    accl_ref[...] = jnp.zeros_like(accl_ref)
+    accm_ref[...] = jnp.zeros_like(accm_ref)
+    accc_ref[...] = jnp.zeros_like(accc_ref)
+    pre_ref[...] = jnp.zeros_like(pre_ref)
+    acc_ref[...] = jnp.zeros_like(acc_ref)
+    sq_ref[...] = jnp.zeros_like(sq_ref)
+
+    def squares(value):
+        value = value.astype(F32)
+        sq_ref[...] += jnp.sum(value * value, axis=1, keepdims=True)
+
+    @pl.when(sec == 0)
+    def _():
         def one(c, carry):
-            value = ref[:, cols(c)].astype(F32) * inverse * gain_ref[:, cols(c)].astype(F32)
-            value = value.astype(BF16)
-            norm_ref[:, cols(c)] = value
-            pin_ref[...] += nt(value, wide_ref[:, cols(c)])
+            value = x_ref[:, cols(c)]
+            squares(value)
+            wide = wide_ref[:, cols(c)].astype(F32) * gain_ref[:, cols(c)].astype(F32)
+            pre_ref[0:t1, 0:rank] += nt(value, wide.astype(BF16))
             return carry
 
         lax.fori_loop(0, chunks, one, 0)
 
-    def projections():
-        acc_ref[...] = jnp.zeros_like(acc_ref)
+    def prepare():
+        give_x.wait_recv()
 
         def one(c, carry):
-            acc_ref[...] += nn(norm_ref[:, cols(c)], g_ref[cols(c), pl.ds(0, 3 * hd)])
+            value = left_ref[0:t1, cols(c)]
+            squares(value)
+            cot = jnp.where(valid, x_ref[:, cols(c)].astype(F32), 0.0).astype(BF16)
+            left_ref[t1:t2, cols(c)] = cot
+            plain = wide_ref[:, cols(c)]
+            wide = plain.astype(F32) * gain_ref[:, cols(c)].astype(F32)
+            left_ref[t2:t3, cols(c)] = plain
+            left_ref[t3:t4, cols(c)] = wide.astype(BF16)
+            pre_ref[0:t2] += nt(left_ref[0:t2, cols(c)], left_ref[t2:t4, cols(c)])
             return carry
 
         lax.fori_loop(0, chunks, one, 0)
+
+    def contract(start, size):
+        start = pl.multiple_of(start, size)
+        span = pl.ds(start, size)
+
+        @pl.when(sec == 0)
+        def _():
+            acc_ref[...] += nn(x_ref[:, span], g_ref[span, pl.ds(0, 3 * hd)])
+
+        @pl.when(sec == 1)
+        def _():
+            wide_w = g_ref[span, pl.ds(0, 3 * hd)]
+            out_w = wo_ref[span]
+            turned = out_w.T
+            left = left_ref[:, span]
+            accl_ref[:, 0 : 3 * hd] += nn(left, wide_w)
+            accl_ref[:, 3 * hd : 4 * hd] += nn(left, out_w)
+            accm_ref[:, 0 : 3 * hd] += nn(turned, wide_w)
+            accm_ref[:, 3 * hd : 4 * hd] += nn(turned, out_w)
+            accc_ref[...] += nn(left_ref[t1:t2, span], g_ref[span, pl.ds(3 * hd, hd)])
+
+    def handed(index):
+        span = pl.ds(pl.multiple_of(at(place - index) * rows, rows), rows)
+
+        @pl.when(sec == 1)
+        def _():
+            across(wo_ref.at[span], wo_ref.at[span], wo_send, wo_recv.at[index]).wait_recv()
+
+    def block(index):
+        if by_block:
+            handed(index)
+            contract(at(place - index) * rows, rows)
+
+    def arrive(s, j):
+        cw(s - 1, j, place - s).wait_recv()
+
+        @pl.when(s < n - 1)
+        def _():
+            cw(s, j, place - s).start()
+
+        over(s, j, place - s, mine).start()
+        offset, size = side[j]
+        hand_over(s, mine + offset, size)
+        ccw(s - 1, j, place + s).wait_recv()
+
+        @pl.when(s < n - 1)
+        def _():
+            ccw(s, j, place + s).start()
+
+        offset, size = middle[j]
+        hand_over(n - s, third + offset, size)
+
+    def take(s, j):
+        over(s, j, place - s, theirs).wait_recv()
+        offset, size = side[j]
+        hand_over(s, theirs + offset, size)
+
+    def step(s, carry):
+        for j in range(parts):
+            arrive(s, j)
+
+            @pl.when(s >= 2)
+            def _():
+                take(s - 1, j)
+
+            if j == 0:
+                @pl.when(s > half + 1)
+                def _():
+                    block(n - s + 1)
+
+            if j == parts - 1:
+                @pl.when(s > half)
+                def _():
+                    block(s - 1)
+
+        @pl.when(s == 2)
+        def _():
+            @pl.when(sec == 1)
+            def _():
+                prepare()
+
+            block(0)
+
+        return carry
+
+    lax.fori_loop(1, n, step, 0)
+    block(1)
+    for j in range(parts):
+        take(n - 1, j)
+    block(n - 1)
+    if not by_block:
+        def wait_for(s, carry):
+            handed(s)
+            return carry
+
+        lax.fori_loop(0, n, wait_for, 0)
+
+        def later(c, carry):
+            contract(c * chunk, chunk)
+            return carry
+
+        lax.fori_loop(0, chunks, later, 0)
 
     def attention():
         q = acc_ref[:, 0:hd].astype(BF16)
@@ -192,43 +327,15 @@
             second = tn(wide_out[span], head_in[span])
             blk_ref[e] = jnp.concatenate([first, second], axis=1).astype(BF16)
 
-    pin_ref[...] = jnp.zeros_like(pin_ref)
+    give_mix = across(mix_ref, mixin_ref, mix_send, mix_recv)
+    give_back = across(back_ref, backin_ref, back_send, back_recv)
+    give_wo = across(wo_ref, wo_ref, wo_send, wo_recv.at[0])
 
     @pl.when(sec == 0)
     def _():
-        normalise(x_ref, rms(x_ref))
-
-    def step(s, carry):
-        cw(s - 1, place - s).wait_recv()
-        cw(s, place - s).start()
-        over(s, place - s, mine).start()
-        hand_over(place - s, mine, third)
-        ccw(s - 1, place + s).wait_recv()
-        ccw(s, place + s).start()
-        hand_over(place + s, third, mid)
-        return carry
-
-    lax.fori_loop(1, n - 1, step, 0)
-    cw(n - 2, place - (n - 1)).wait_recv()
-    over(n - 1, place - (n - 1), mine).start()
-    hand_over(place - (n - 1), mine, third)
-    ccw(n - 2, place + n - 1).wait_recv()
-    hand_over(place + n - 1, third, mid)
-
-    def take(s, carry):
-        over(s, place - s, theirs).wait_recv()
-        hand_over(place - s, theirs, third)
-        return carry
-
-    lax.fori_loop(1, n, take, 0)
-
-    give_mix = across(mix_ref, mixin_ref, mix_send, mix_recv)
-    give_back = across(back_ref, backin_ref, back_send, back_recv)
-    give_wo = across(wo_ref, wo_ref, wo_send, wo_recv)
-
-    @pl.when(sec == 0)
-    def _():
-        projections()
+        inverse = lax.rsqrt(sq_ref[...] / width + EPSILON)
+        acc_ref[...] = acc_ref[...] * inverse
+        pin_ref[...] = pre_ref[0:t1, 0:rank] * inverse
         _, _, _, probs, mixed = attention()
         mix_ref[...] = mixed
         give_mix.start()
@@ -244,33 +351,18 @@
 
     @pl.when(sec == 1)
     def _():
-        acc_ref[...] = jnp.zeros_like(acc_ref)
-
-        def early(c, carry):
-            cot = jnp.where(valid, x_ref[:, cols(c)].astype(F32), 0.0).astype(BF16)
-            acc_ref[:, 0:hd] += nn(cot, g_ref[cols(c), pl.ds(3 * hd, hd)])
-            acc_ref[:, hd : hd + rank] += nt(cot, wide_ref[:, cols(c)])
-            return carry
-
-        lax.fori_loop(0, chunks, early, 0)
-        dmixed = acc_ref[:, 0:hd].astype(BF16)
-        wide_out = acc_ref[:, hd : hd + rank].astype(BF16)
-        give_x.wait_recv()
-        give_wo.wait_recv()
+        dmixed = accc_ref[...].astype(BF16)
+        plain_out = pre_ref[t1:t2, 0:rank]
         give_mix.wait_recv()
         before = mixin_ref[...]
-
-        def advance(c, total):
-            value = far_ref[:, cols(c)].astype(F32) + nt(before, wo_ref[cols(c), :])
-            value = value.astype(BF16)
-            mid_ref[:, cols(c)] = value
-            value = value.astype(F32)
-            return total + jnp.sum(value * value, axis=1, keepdims=True)
-
-        total = lax.fori_loop(0, chunks, advance, jnp.zeros((tokens, 1), F32))
-        inverse = lax.rsqrt(total / width + EPSILON)
-        normalise(mid_ref, inverse)
-        projections()
+        moved = nn(before, accm_ref[...].astype(BF16))
+        tilted = accl_ref[0:t1, 3 * hd : 4 * hd]
+        square = moved[:, 3 * hd : 4 * hd] + 2.0 * tilted
+        total = sq_ref[...] + jnp.sum(before.astype(F32) * square, axis=1, keepdims=True)
+        inverse = lax.rsqrt(jnp.maximum(total, 0.0) / width + EPSILON)
+        acc_ref[...] = (accl_ref[0:t1, 0 : 3 * hd] + moved[:, 0 : 3 * hd]) * inverse
+        turned = nt(before, accl_ref[t2:t4, 3 * hd : 4 * hd].astype(BF16))
+        pin_ref[...] = (pre_ref[0:t1, rank : 2 * rank] + turned[:, rank : 2 * rank]) * inverse
         q, k, v, probs, mixed = attention()
         rounded = probs.astype(BF16)
         dvalue = tn(rounded, dmixed).astype(BF16)
@@ -282,22 +374,17 @@
         dall = jnp.concatenate([dq, dk, dvalue], axis=1)
         share = jnp.sum(dall.astype(F32) * acc_ref[...], axis=1, keepdims=True)
         share = share * inverse * inverse / width
-        acc_ref[...] = jnp.zeros_like(acc_ref)
-
-        def retreat(c, carry):
-            dnorm = nt(dall, g_ref[cols(c), pl.ds(0, 3 * hd)])
-            cot = jnp.where(valid, x_ref[:, cols(c)].astype(F32), 0.0)
-            cot = cot + dnorm * inverse * gain_ref[:, cols(c)].astype(F32)
-            cot = (cot - mid_ref[:, cols(c)].astype(F32) * share).astype(BF16)
-            acc_ref[:, 0:hd] += nn(cot, wo_ref[cols(c), :])
-            acc_ref[:, hd : hd + rank] += nt(cot, wide_ref[:, cols(c)])
-            return carry
-
-        lax.fori_loop(0, chunks, retreat, 0)
-        back_ref[:, 0:hd] = acc_ref[:, 0:hd].astype(BF16)
-        back_ref[:, hd : 2 * hd] = jnp.where(valid, acc_ref[:, hd : 2 * hd], 0.0).astype(BF16)
+        to_head = inverse * nt(dall, accm_ref[:, 0 : 3 * hd].astype(BF16))
+        to_head = to_head - share * (tilted + moved[:, 3 * hd : 4 * hd])
+        to_head = to_head + accl_ref[t1:t2, 3 * hd : 4 * hd]
+        to_wide = inverse * nt(dall, accl_ref[t2:t3, 0 : 3 * hd].astype(BF16))
+        to_wide = to_wide - share * (pre_ref[0:t1, 0:rank] + turned[:, 0:rank])
+        to_wide = jnp.where(valid, to_wide + plain_out, 0.0)
+        back_ref[:, 0:hd] = to_head.astype(BF16)
+        back_ref[:, hd : hd + rank] = to_wide.astype(BF16)
+        back_ref[:, hd + rank : 2 * hd] = jnp.zeros((tokens, hd - rank), BF16)
         give_back.start()
-        finish(mixed, dvalue, wide_out)
+        finish(mixed, dvalue, plain_out.astype(BF16))
         give_back.wait_send()
 
     def spread(i, carry):
@@ -341,9 +428,10 @@
     shared.wait_send()
 
     def drain(s, carry):
-        cw(s, place).wait_send()
-        ccw(s, place).wait_send()
-        over(s + 1, place, mine).wait_send()
+        for j in range(parts):
+            cw(s, j, place).wait_send()
+            ccw(s, j, place).wait_send()
+            over(s + 1, j, place, mine).wait_send()
         return carry
 
     lax.fori_loop(0, n - 1, drain, 0)
@@ -357,15 +445,18 @@
     rows, hd = w_query.shape[1:]
     rank = proj_wide.shape[0]
     tokens = examples * length
-    chunk = min(width, 1024)
-    weights = jnp.concatenate([w_query[0], w_key[0], w_value[0], w_out[0].T], axis=1)
+    parts = 2 if rows >= 128 else 1
+    gain = lax.dynamic_slice_in_dim(norm_gain[0], lax.axis_index("dp") * rows, rows)
+    weights = jnp.concatenate([w_query[0], w_key[0], w_value[0]], axis=1)
+    weights = (weights.astype(F32) * gain.astype(F32)[:, None]).astype(BF16)
+    weights = jnp.concatenate([weights, w_out[0].T], axis=1)
     padded = -(-examples // 8) * 8
     own = jnp.pad(owners, ((0, padded - examples), (0, 0)))
     own = jnp.broadcast_to(own, (padded, 2 * rank))
     vmem = pl.BlockSpec(memory_space=pltpu.VMEM)
     dma = pltpu.SemaphoreType.DMA
     out = pl.pallas_call(
-        functools.partial(kernel, n, examples, length, chunk),
+        functools.partial(kernel, n, examples, length, parts),
         out_shape=jax.ShapeDtypeStruct((CAP, 2, rank, rank), BF16),
         in_specs=[
             pl.BlockSpec(memory_space=pltpu.SMEM), pl.BlockSpec(memory_space=pl.ANY),
@@ -375,10 +466,13 @@
         scratch_shapes=[
             pltpu.VMEM((width, 4 * hd), BF16),
             pltpu.VMEM((width, hd), BF16),
-            pltpu.VMEM((tokens, width), BF16),
-            pltpu.VMEM((tokens, width), BF16),
-            pltpu.VMEM((tokens, width), BF16),
+            pltpu.VMEM((2 * tokens + 2 * rank, width), BF16),
+            pltpu.VMEM((2 * tokens + 2 * rank, 4 * hd), F32),
+            pltpu.VMEM((hd, 4 * hd), F32),
+            pltpu.VMEM((tokens, hd), F32),
+            pltpu.VMEM((2 * tokens, 2 * rank), F32),
             pltpu.VMEM((tokens, 3 * hd), F32),
+            pltpu.VMEM((tokens, 1), F32),
             pltpu.VMEM((tokens, rank), F32),
             pltpu.VMEM((tokens, tokens), BF16),
             pltpu.VMEM((tokens, hd), BF16),
@@ -389,7 +483,7 @@
             pltpu.VMEM((n, examples, rank, 2 * rank), BF16),
             pltpu.VMEM((n, padded, 2 * rank), jnp.int32),
             pltpu.VMEM((CAP, rank, 2 * rank), F32),
-            dma, dma, dma((n,)), dma((n,)), dma((n,)), dma, dma,
+            dma, dma, dma((n * parts,)), dma((n * parts,)), dma((n * parts,)), dma, dma((n,)),
             dma, dma, dma, dma, dma, dma,
             dma, dma, dma, dma,
         ],

time: 102 us -> 86.4 us (0.85)
  Pallas kernels: 96.3 us -> 80.6 us
    pallas_call x1, Pallas kernels: 96.3 us -> 80.6 us  [shards(): pl.pallas_call(functools.partial(kernel, n, examples, length, parts), out...]
    convert_element_type x0 -> x2, other arithmetic: none -> 2.04 us  [shards(): weights = (weights.astype(F32) * gain.astype(F32)[:, None]).astype(BF16)]
    concatenate x1, other arithmetic: 2.21 us -> 1.08 us  [shards(): weights = jnp.concatenate([weights, w_out[0].T], axis=1)]
    unnamed x4 -> x6, local copies, waits for them, and re-layouts: 2.7 us -> 1.75 us
where the time goes in v2:
time: 86.4 us; the launch traced here: 86.2 us
  Pallas kernels  80.6 us (93%)
  other arithmetic  3.12 us (4%)
  local copies, waits for them, and re-layouts  2.42 us (3%)
    pallas_call x1, Pallas kernels, shards(): pl.pallas_call(functools.partial(kernel, n, examples, length, parts), out...  80.6 us
    convert_element_type x2, other arithmetic, shards(): weights = (weights.astype(F32) * gain.astype(F32)[:, None]).astype(BF16)  2.04 us
    unnamed x6, local copies, waits for them, and re-layouts  1.75 us

profile of v2, /device:TPU:0, one launch (start us, length us, event | category | flops | bytes accessed | tf_op | source)
XLA Modules:
  0.0 86.2 jit_solution(5384362753616766072)
XLA Ops:
  0.0 0.0 copy-start
  0.0 0.7 dynamic-slice_convert_fusion
  0.7 1.3 %multiply_convert_fusion = bf16[1024,384]{1,0:T(8,128)(2,1)S(1)} fusion(bf16[1024,128]{1,0:T(8,128)(2,1)} %bitcast.17, bf16[1024,128]{1,0:T(8,128)(2,1)} %bitcast.18, bf16[1024,128]{1,0:T(8,128)(2,1)} %bitcast.19, f32[1024]{0:T(1024)S(1)} %bitcast.21), kind=kLoop, calls=%fused_computation | loop fusion | flops 3145728 | bytes 1576960 | tf_op jit(solution)/shard_map/convert_element_type | solution.py:451
  2.1 0.0 copy-done
  2.1 0.0 copy-start.1
  2.1 0.2 copy.11
  2.3 1.1 %pad_maximum_fusion.w_ref = bf16[1024,512]{1,0:T(8,128)(2,1)} fusion(bf16[1024,128]{1,0:T(8,128)(2,1)S(1)} %bitcast.15, bf16[1024,384]{1,0:T(8,128)(2,1)S(1)} %multiply_convert_fusion), kind=kLoop, calls=%fused_computation.1 | loop fusion | flops 2097152 | bytes 2097152 | tf_op jit(solution)/shard_map/concatenate | solution.py:452
  3.3 0.0 copy-done.1
  3.3 0.7 broadcast_in_dim.12.own_ref
  4.0 80.6 %shard_map.100 = bf16[4,2,64,64]{3,2,1,0:T(8,128)(2,1)} custom-call(s32[2]{0:T(128)} %len_ref.1, bf16[1024,512]{1,0:T(8,128)(2,1)} %pad_maximum_fusion.w_ref, bf16[128,8192]{1,0:T(8,128)(2,1)} %bitcast.14, bf16[1,8192]{1,0:T(2,128)(2,1)} %gain_ref.1, bf16[64,8192]{1,0:T(8,128)(2,1)} %wide_ref.1, bf16[2,64,128]{2,1,0:T(8,128)(2,1)} %bitcast.20, ...), custom_call_target="tpu_custom_call" | custom-call | tf_op jit(solution)/shard_map/pallas_call | solution.py:458
  84.6 1.6 %copy.14 = bf16[4,1,2,64,64]{4,3,2,1,0:T(8,128)(2,1)} copy(bf16[4,1,2,64,64]{4,3,2,1,0:T(8,128)(2,1)} %bitcast.16) | data formatting | bytes 131072
  (1 shorter events, 0.0 us)
Async XLA Ops:
  0.0 2.1 %copy-start = (bf16[1,128,1024]{2,1,0:T(8,128)(2,1)S(1)}, bf16[1,128,1024]{2,1,0:T(8,128)(2,1)}, u32[]{:S(2)}) copy-start(bf16[1,128,1024]{2,1,0:T(8,128)(2,1)} %param.14) | copy-start | bytes 786436
  2.1 1.3 %copy-start.1 = (s32[2,1]{0,1:T(1,128)S(1)}, s32[2,1]{0,1:T(1,128)}, u32[]{:S(2)}) copy-start(s32[2,1]{0,1:T(1,128)} %param.19) | copy-start | bytes 28

commit v3 on v2

--- a/solution.py
+++ b/solution.py
@@ -29,19 +29,20 @@
 
 def kernel(
     n, examples, length, parts,
-    len_ref, w_ref, x_ref, gain_ref, wide_ref, head_ref, own_ref,
+    len_ref, owner_ref, wq_ref, wk_ref, wv_ref, wt_ref, near_ref, x_ref, gain_ref, wide_ref,
+    head_ref,
     out_ref,
     g_ref, wo_ref, left_ref, accl_ref, accm_ref, accc_ref, pre_ref, acc_ref, sq_ref,
     pin_ref, prb_ref, mix_ref, back_ref, mixin_ref, backin_ref, blk_ref, all_ref,
-    own_all, pick_ref,
-    loc_sem, send_sem, cw_sem, ccw_sem, y_sem, wo_send, wo_recv,
+    own_ref, own_all, pick_ref,
+    send_sem, cw_sem, ccw_sem, y_sem, wo_send, wo_recv,
     x_send, x_recv, mix_send, mix_recv, back_send, back_recv,
     own_send, own_recv, blk_send, blk_recv,
 ):
     group = lax.axis_index("groups")
     me = lax.axis_index("dp")
     sec = lax.axis_index("section")
-    rows = w_ref.shape[0]
+    rows = wq_ref.shape[0]
     tokens, width = x_ref.shape
     hd = wo_ref.shape[1]
     rank = wide_ref.shape[0]
@@ -76,12 +77,19 @@
         )
         return carry
 
-    own_block = pltpu.make_async_copy(w_ref, g_ref.at[pl.ds(me * rows, rows)], loc_sem)
-    own_block.start()
     lax.fori_loop(1, n, greet, 0)
     pl.semaphore_signal(barrier, inc=1, device_id={"groups": 1 - group}, device_id_type=MESH)
     pl.semaphore_signal(barrier, inc=1, device_id={"section": 1 - sec}, device_id_type=MESH)
-    own_block.wait()
+    base = pl.ds(pl.multiple_of(me * rows, rows), rows)
+    by_block = rows % 128 == 0
+    near = near_ref[:, base] if by_block else near_ref[...]
+    near = jnp.broadcast_to(near.astype(F32), (hd, rows)).T
+    for m, ref in enumerate((wq_ref, wk_ref, wv_ref)):
+        g_ref[base, m * hd : (m + 1) * hd] = (ref[...].astype(F32) * near).astype(BF16)
+    g_ref[base, 3 * hd : 4 * hd] = wt_ref[...].T
+    own_ref[...] = jnp.zeros_like(own_ref)
+    for e in range(examples):
+        own_ref[e : e + 1] = jnp.full((1, 2 * rank), owner_ref[e, 0], jnp.int32)
     pl.semaphore_wait(barrier, n + 1)
 
     def part(origin, offset, size):
@@ -160,7 +168,6 @@
     scale = hd ** (-0.5)
     chunk = min(width, 1024)
     chunks = width // chunk
-    by_block = rows % 128 == 0
     t1, t2, t3, t4 = tokens, 2 * tokens, 2 * tokens + rank, 2 * tokens + 2 * rank
 
     def cols(c):
@@ -446,21 +453,18 @@
     rank = proj_wide.shape[0]
     tokens = examples * length
     parts = 2 if rows >= 128 else 1
-    gain = lax.dynamic_slice_in_dim(norm_gain[0], lax.axis_index("dp") * rows, rows)
-    weights = jnp.concatenate([w_query[0], w_key[0], w_value[0]], axis=1)
-    weights = (weights.astype(F32) * gain.astype(F32)[:, None]).astype(BF16)
-    weights = jnp.concatenate([weights, w_out[0].T], axis=1)
+    near = norm_gain
+    if rows % 128:
+        near = lax.dynamic_slice_in_dim(near, lax.axis_index("dp") * rows, rows, axis=1)
     padded = -(-examples // 8) * 8
-    own = jnp.pad(owners, ((0, padded - examples), (0, 0)))
-    own = jnp.broadcast_to(own, (padded, 2 * rank))
     vmem = pl.BlockSpec(memory_space=pltpu.VMEM)
+    smem = pl.BlockSpec(memory_space=pltpu.SMEM)
     dma = pltpu.SemaphoreType.DMA
     out = pl.pallas_call(
         functools.partial(kernel, n, examples, length, parts),
         out_shape=jax.ShapeDtypeStruct((CAP, 2, rank, rank), BF16),
         in_specs=[
-            pl.BlockSpec(memory_space=pltpu.SMEM), pl.BlockSpec(memory_space=pl.ANY),
-            vmem, vmem, vmem, vmem, vmem,
+            smem, smem, vmem, vmem, vmem, vmem, vmem, vmem, vmem, vmem, vmem,
         ],
         out_specs=vmem,
         scratch_shapes=[
@@ -481,9 +485,10 @@
             pltpu.VMEM((tokens, 2 * hd), BF16),
             pltpu.VMEM((examples, rank, 2 * rank), BF16),
             pltpu.VMEM((n, examples, rank, 2 * rank), BF16),
+            pltpu.VMEM((padded, 2 * rank), jnp.int32),
             pltpu.VMEM((n, padded, 2 * rank), jnp.int32),
             pltpu.VMEM((CAP, rank, 2 * rank), F32),
-            dma, dma, dma((n * parts,)), dma((n * parts,)), dma((n * parts,)), dma, dma((n,)),
+            dma, dma((n * parts,)), dma((n * parts,)), dma((n * parts,)), dma, dma((n,)),
             dma, dma, dma, dma, dma, dma,
             dma, dma, dma, dma,
         ],
@@ -491,8 +496,8 @@
             collective_id=0, has_side_effects=True, vmem_limit_bytes=56 * 1024 * 1024
         ),
     )(
-        lengths, weights, boundary.reshape(tokens, width), norm_gain,
-        proj_wide, proj_head[0], own,
+        lengths, owners, w_query[0], w_key[0], w_value[0], w_out[0], near,
+        boundary.reshape(tokens, width), norm_gain, proj_wide, proj_head[0],
     )
     return out[:, None]
 

time: 86.4 us -> 83.7 us (0.969)
  other arithmetic: 3.12 us -> 0 us
    convert_element_type x2 -> x0, other arithmetic: 2.04 us -> none  [shards(): weights = (weights.astype(F32) * gain.astype(F32)[:, None]).astype(BF16)]
    unnamed x6 -> x2, local copies, waits for them, and re-layouts: 1.75 us -> 2.86 us
    concatenate x1 -> x0, other arithmetic: 1.08 us -> none  [shards(): weights = jnp.concatenate([weights, w_out[0].T], axis=1)]
where the time goes in v3:
time: 83.7 us; the launch traced here: 83.6 us
  Pallas kernels  80.7 us (96%)
  local copies, waits for them, and re-layouts  2.86 us (3%)
    pallas_call x1, Pallas kernels, shards(): pl.pallas_call(functools.partial(kernel, n, examples, length, parts), out...  80.7 us
    unnamed x2, local copies, waits for them, and re-layouts  2.86 us

profile of v3, /device:TPU:0, one launch (start us, length us, event | category | flops | bytes accessed | tf_op | source)
XLA Modules:
  0.0 83.6 jit_solution(205508406037745022)
XLA Ops:
  0.0 1.3 %copy.11.owner_ref = s32[2,1]{1,0:T(2,128)} copy(s32[2,1]{0,1:T(1,128)} %param.19) | data formatting | bytes 16 | tf_op args[9]
  1.3 80.7 %shard_map.100 = bf16[4,2,64,64]{3,2,1,0:T(8,128)(2,1)} custom-call(s32[2]{0:T(128)} %len_ref.1, s32[2,1]{1,0:T(2,128)} %copy.11.owner_ref, bf16[1024,128]{1,0:T(8,128)(2,1)} %bitcast.11, bf16[1024,128]{1,0:T(8,128)(2,1)} %bitcast.12, bf16[1024,128]{1,0:T(8,128)(2,1)} %bitcast.13, bf16[128,1024]{1,0:T(8,128)(2,1)} %bitcast.14, bf16[1,8192]{1,0:T(2,128)(2,1)} %gain_ref.1, ...), custom_call_target="tpu_custom_call" | custom-call | tf_op jit(solution)/shard_map/pallas_call | solution.py:463
  82.0 1.6 %copy.14 = bf16[4,1,2,64,64]{4,3,2,1,0:T(8,128)(2,1)} copy(bf16[4,1,2,64,64]{4,3,2,1,0:T(8,128)(2,1)} %bitcast.10) | data formatting | bytes 131072

commit v4 on v3

--- a/solution.py
+++ b/solution.py
@@ -89,7 +89,7 @@
     g_ref[base, 3 * hd : 4 * hd] = wt_ref[...].T
     own_ref[...] = jnp.zeros_like(own_ref)
     for e in range(examples):
-        own_ref[e : e + 1] = jnp.full((1, 2 * rank), owner_ref[e, 0], jnp.int32)
+        own_ref[e : e + 1] = jnp.full((1, 2 * rank), owner_ref[0, e], jnp.int32)
     pl.semaphore_wait(barrier, n + 1)
 
     def part(origin, offset, size):
@@ -496,7 +496,7 @@
             collective_id=0, has_side_effects=True, vmem_limit_bytes=56 * 1024 * 1024
         ),
     )(
-        lengths, owners, w_query[0], w_key[0], w_value[0], w_out[0], near,
+        lengths, owners.T, w_query[0], w_key[0], w_value[0], w_out[0], near,
         boundary.reshape(tokens, width), norm_gain, proj_wide, proj_head[0],
     )
     return out[:, None]

time: 83.7 us -> 82.4 us (0.984)
  local copies, waits for them, and re-layouts: 2.86 us -> 1.57 us
    unnamed x2 -> x1, local copies, waits for them, and re-layouts: 2.86 us -> 1.57 us
where the time goes in v4:
time: 82.4 us; the launch traced here: 82.3 us
  Pallas kernels  80.7 us (98%)
  local copies, waits for them, and re-layouts  1.57 us (2%)
    pallas_call x1, Pallas kernels, shards(): pl.pallas_call(functools.partial(kernel, n, examples, length, parts), out...  80.7 us

profile of v4, /device:TPU:0, one launch (start us, length us, event | category | flops | bytes accessed | tf_op | source)
XLA Modules:
  0.0 82.3 jit_solution(14670251526170253640)
XLA Ops:
  0.0 80.7 %shard_map.100 = bf16[4,2,64,64]{3,2,1,0:T(8,128)(2,1)} custom-call(s32[2]{0:T(128)} %len_ref.1, s32[1,2]{1,0:T(1,128)} %bitcast.17, bf16[1024,128]{1,0:T(8,128)(2,1)} %bitcast.12, bf16[1024,128]{1,0:T(8,128)(2,1)} %bitcast.13, bf16[1024,128]{1,0:T(8,128)(2,1)} %bitcast.14, bf16[128,1024]{1,0:T(8,128)(2,1)} %bitcast.15, bf16[1,8192]{1,0:T(2,128)(2,1)} %gain_ref.1, ...), custom_call_target="tpu_custom_call" | custom-call | tf_op jit(solution)/shard_map/pallas_call | solution.py:463
  80.7 1.6 %copy.13 = bf16[4,1,2,64,64]{4,3,2,1,0:T(8,128)(2,1)} copy(bf16[4,1,2,64,64]{4,3,2,1,0:T(8,128)(2,1)} %bitcast.11) | data formatting | bytes 131072
